TPU v7x, 32 devices: a whole 2x2x4 slice. The times are simulated.
32 devices in a mesh: section: 4 (over x, core), dp: 2 (over y), ctx: 4 (over z).
Axes of the slice: x: 2, y: 2, z: 4, core: 2. Of those that a mesh axis runs over, the one named last changes fastest.
Arguments:
- layer_input: bfloat16 [4, 2, 512, 4096], P('section', 'dp', 'ctx'), may hold values from -6 to 6
- attn_grad: bfloat16 [4, 2, 512, 4096], P('section', 'dp', 'ctx'), may hold values from -48 to 48
- queries: bfloat16 [4, 2, 512, 4096], P('section', 'dp', None, 'ctx'), may hold values from -6 to 6
- keys: bfloat16 [4, 2, 512, 512], P('section', 'dp', 'ctx'), may hold values from -6 to 6
- values: bfloat16 [4, 2, 512, 512], P('section', 'dp', 'ctx'), may hold values from -4 to 4
- kv_weight: bfloat16 [4, 4096, 1024], P('section', 'ctx'), may hold values from -0.09375 to 0.09375
- segments: int32 [2, 512], P('dp'), may hold values from 0 to 3, as said below
- positions: int32 [2, 512], P('dp'), may hold values from 0 to 16383, as said below
Outputs:
- grad_prev: bfloat16 [4, 2, 512, 4096], P('section', 'dp', 'ctx')
- query_grad: bfloat16 [4, 2, 512, 4096], P('section', 'dp', 'ctx')
- weight_grad: float32 [4, 4096, 1024], P('section', 'ctx', 'dp')
Inputs may be any that keep to these rules, and one draw needn't show every extreme that they name: `segments`: every sequence holds four documents: segment ids start at 0, never fall, and end at 3. Inside a segment positions rise by one a token.
All inputs are finite; a program needn't handle non-finite values.
Results may differ from a plain program's by a relative error of at most 0.012.
Values may be sent and summed in bfloat16 or wider, within the bound.
No kernel may reach another device: no remote copies, remote signals or barrier semaphores. Data moves between devices by JAX's collectives and lax.ppermute only.
A program may use at most 128 MiB of HBM per device.

v0:
```python
import math
import jax
import jax.numpy as jnp
import numpy as np
from jax import lax
from jax.sharding import PartitionSpec as P

QUERY_HEADS = 32
KEY_VALUE_HEADS = 4
HEAD_WIDTH = 128


def passed_along(value, axis, by):
    size = lax.axis_size(axis)
    pairs = [(i, i + by) for i in range(size) if 0 <= i + by < size]
    return lax.ppermute(value, axis, pairs)


def yarn_table(head_size):
    theta_base = 1000000.0
    factor = 4.0
    pretrain_len = 32768.0
    exponent = np.arange(0, head_size, 2) / head_size
    extrapolated = 1.0 / theta_base**exponent
    interpolated = extrapolated / factor

    def boundary(rotations):
        return (
            head_size
            * math.log(pretrain_len / (rotations * 2.0 * math.pi))
            / (2.0 * math.log(theta_base))
        )

    lower_dim = max(math.floor(boundary(32.0)), 0)
    upper_dim = min(math.ceil(boundary(1.0)), head_size - 1)
    ramp_width = max(upper_dim - lower_dim, 0.001)
    ramp_share = np.clip((np.arange(head_size // 2) - lower_dim) / ramp_width, 0.0, 1.0)
    keep_share = 1.0 - ramp_share
    frequency = interpolated * (1.0 - keep_share) + extrapolated * keep_share
    return (frequency.astype(np.float32), float(0.1 * math.log(factor) + 1.0))


def rotate_back(gradient, places, frequency, mscale):
    angles = places.astype(jnp.float32)[:, None] * frequency[None, :]
    cosine = jnp.cos(angles) * mscale
    sine_term = jnp.sin(angles) * mscale
    cosine = jnp.concatenate([cosine, cosine], -1)[:, None, :]
    sine_term = jnp.concatenate([sine_term, sine_term], -1)[:, None, :]
    half_size = gradient.shape[-1] // 2
    turned = jnp.concatenate([gradient[..., half_size:], -gradient[..., :half_size]], -1)
    return gradient * cosine + turned * sine_term


def attend_local(query_heads, key_heads, value_heads, grad_heads, seg_ids):
    sequence_length = query_heads.shape[0]
    local_heads = query_heads.shape[1] // HEAD_WIDTH
    kv_heads = key_heads.shape[1] // HEAD_WIDTH
    group_share_count = local_heads // kv_heads
    score_scale = HEAD_WIDTH ** (-0.5)
    query_complete = query_heads.reshape(sequence_length, kv_heads, group_share_count, HEAD_WIDTH)
    key_complete = key_heads.reshape(sequence_length, kv_heads, HEAD_WIDTH)
    value_complete = value_heads.reshape(sequence_length, kv_heads, HEAD_WIDTH)
    gradient_total = grad_heads.reshape(sequence_length, kv_heads, group_share_count, HEAD_WIDTH)
    block_rows = min(512, sequence_length)
    dq_parts = []
    key_gradient = jnp.zeros((sequence_length, kv_heads, HEAD_WIDTH), jnp.float32)
    value_gradient = jnp.zeros((sequence_length, kv_heads, HEAD_WIDTH), jnp.float32)
    for block_index in range(sequence_length // block_rows):
        row_start = block_index * block_rows
        row_stop = row_start + block_rows
        q_blk = query_complete[row_start:row_stop]
        k_blk = key_complete[:row_stop]
        v_blk = value_complete[:row_stop]
        g_blk = gradient_total[row_start:row_stop]
        scores = (
            jnp.einsum("qkgd,lkd->kgql", q_blk, k_blk, preferred_element_type=jnp.float32)
            * score_scale
        )
        row_ids = jnp.arange(row_start, row_stop)[:, None]
        col_ids = jnp.arange(row_stop)[None, :]
        allowed = (col_ids <= row_ids) & (
            seg_ids[row_start:row_stop][:, None] == seg_ids[:row_stop][None, :]
        )
        scores = jnp.where(allowed, scores, -1e30)
        row_max = jnp.max(scores, -1, keepdims=True)
        shifted = jnp.exp(scores - row_max)
        row_total = jnp.sum(shifted, -1, keepdims=True)
        attention = shifted / row_total
        probs_half = attention.astype(jnp.bfloat16)
        outputs = jnp.einsum(
            "kgql,lkd->qkgd", probs_half, v_blk, preferred_element_type=jnp.float32
        )
        row_delta = jnp.transpose(jnp.sum(g_blk.astype(jnp.float32) * outputs, -1), (1, 2, 0))[
            ..., None
        ]
        dprobs = jnp.einsum("qkgd,lkd->kgql", g_blk, v_blk, preferred_element_type=jnp.float32)
        dscore_half = (attention * (dprobs - row_delta)).astype(jnp.bfloat16)
        dq_parts.append(
            jnp.einsum("kgql,lkd->qkgd", dscore_half, k_blk, preferred_element_type=jnp.float32)
            * score_scale
        )
        key_gradient = key_gradient.at[:row_stop].add(
            jnp.einsum("kgql,qkgd->lkd", dscore_half, q_blk, preferred_element_type=jnp.float32)
            * score_scale
        )
        value_gradient = value_gradient.at[:row_stop].add(
            jnp.einsum("kgql,qkgd->lkd", probs_half, g_blk, preferred_element_type=jnp.float32)
        )
    query_grad = jnp.concatenate(dq_parts, 0).reshape(sequence_length, local_heads, HEAD_WIDTH)
    return (query_grad, key_gradient, value_gradient)


def on_device(layer_input, attn_grad, queries, keys, values, kv_weight, segments, positions):
    frequency, mscale = yarn_table(HEAD_WIDTH)
    inputs = layer_input[0, 0]
    output_gradient = attn_grad[0, 0]
    query_heads = queries[0, 0]
    key_row_block = keys[0, 0]
    value_row_block = values[0, 0]
    weight_rows = kv_weight[0]
    seg_ids = segments[0]
    places = positions[0]
    ctx_size = lax.axis_size("ctx")
    ctx_index = lax.axis_index("ctx")
    data_size = lax.axis_size("dp")
    sequence_length = query_heads.shape[0]
    kv_width = key_row_block.shape[1]
    kv_heads = kv_width // HEAD_WIDTH
    local_heads = query_heads.shape[1] // HEAD_WIDTH
    group_share_count = QUERY_HEADS // KEY_VALUE_HEADS
    kv_local = max(1, kv_heads // ctx_size)
    grad_heads = lax.all_to_all(output_gradient, "ctx", split_axis=1, concat_axis=0, tiled=True)
    key_complete, value_complete = (
        lax.all_gather(key_row_block, "ctx", axis=0, tiled=True),
        lax.all_gather(value_row_block, "ctx", axis=0, tiled=True),
    )
    first_col = ctx_index * local_heads // group_share_count * HEAD_WIDTH
    key_heads = lax.dynamic_slice_in_dim(key_complete, first_col, kv_local * HEAD_WIDTH, 1)
    value_heads = lax.dynamic_slice_in_dim(value_complete, first_col, kv_local * HEAD_WIDTH, 1)
    query_grad, key_gradient, value_gradient = attend_local(
        query_heads, key_heads, value_heads, grad_heads, seg_ids
    )
    query_back = (
        rotate_back(query_grad, places, frequency, mscale)
        .astype(jnp.bfloat16)
        .reshape(sequence_length, local_heads * HEAD_WIDTH)
    )
    query_out = lax.all_to_all(query_back, "ctx", split_axis=0, concat_axis=1, tiled=True)
    key_back = rotate_back(key_gradient, places, frequency, mscale).reshape(
        sequence_length, kv_local * HEAD_WIDTH
    )
    value_back = value_gradient.reshape(sequence_length, kv_local * HEAD_WIDTH)
    zeros_full = jnp.zeros((sequence_length, kv_width), jnp.float32)
    key_full = lax.dynamic_update_slice_in_dim(zeros_full, key_back, first_col, 1)
    value_full = lax.dynamic_update_slice_in_dim(zeros_full, value_back, first_col, 1)
    key_sum, value_sum = (
        lax.psum_scatter(key_full, "ctx", scatter_dimension=0, tiled=True),
        lax.psum_scatter(value_full, "ctx", scatter_dimension=0, tiled=True),
    )
    kv_grad = jnp.concatenate([key_sum, value_sum], 1).astype(jnp.bfloat16)
    input_cols = lax.all_to_all(inputs, "ctx", split_axis=1, concat_axis=0, tiled=True)
    gradient_total = lax.all_gather(kv_grad, "ctx", axis=0, tiled=True)
    rows_part = jnp.einsum(
        "td,tc->dc", input_cols, gradient_total, preferred_element_type=jnp.float32
    )
    cols_back = jnp.einsum(
        "tc,rc->tr", gradient_total, weight_rows, preferred_element_type=jnp.float32
    ).astype(jnp.bfloat16)
    back_rows = lax.all_to_all(cols_back, "ctx", split_axis=0, concat_axis=1, tiled=True)
    weight_grad = lax.psum_scatter(rows_part, "dp", scatter_dimension=1, tiled=True) / data_size
    grad_prev = passed_along(back_rows, "section", -1)
    return (grad_prev[None, None], query_out[None, None], weight_grad[None])


def solution(mesh):
    return jax.shard_map(
        on_device,
        mesh=mesh,
        in_specs=(
            P("section", "dp", "ctx", None),
            P("section", "dp", "ctx", None),
            P("section", "dp", None, "ctx"),
            P("section", "dp", "ctx", None),
            P("section", "dp", "ctx", None),
            P("section", "ctx", None),
            P("dp", None),
            P("dp", None),
        ),
        out_specs=(
            P("section", "dp", "ctx", None),
            P("section", "dp", "ctx", None),
            P("section", "ctx", "dp"),
        ),
        check_vma=False,
    )
```

profile of v0, /device:TPU:0, one launch (start us, length us, event | category | flops | bytes accessed | tf_op | source)
XLA Modules:
  0.0 270.1 jit_solution(15797264139231069279)
XLA Ops:
  7.2 2.0 all_to_all.50
  9.2 1.3 copy.78
  10.5 6.3 %all-to-all-start = ((bf16[128,4,1024]{2,0,1:T(8,128)(2,1)}), bf16[128,4,1024]{2,0,1:T(8,128)(2,1)S(1)}, u32[]{:S(2)}, u32[]{:S(2)}) async-start(bf16[128,4,1024]{2,0,1:T(8,128)(2,1)} %copy.78), calls=%async_computation | async-start | bytes 2097152 | tf_op jit(solution)/shard_map/all_to_all | solution.py:132
  16.8 2.3 copy.108
  19.1 34.3 %all-gather = bf16[1,1,512,512]{3,2,1,0:T(8,128)(2,1)} all-gather(bf16[1,1,128,512]{3,2,1,0:T(8,128)(2,1)S(1)} %copy-done.10), channel_id=2, replica_groups=mesh['section'=4,'dp'=2,'ctx'=4] {'ctx'}, dimensions={2}, use_global_device_ids=true | all-gather | bytes 655360 | tf_op jit(solution)/shard_map/all_gather | solution.py:134
  53.4 16.6 %all-gather.1 = bf16[1,1,512,512]{3,2,1,0:T(8,128)(2,1)} all-gather(bf16[1,1,128,512]{3,2,1,0:T(8,128)(2,1)S(1)} %copy-done.11), channel_id=3, replica_groups=mesh['section'=4,'dp'=2,'ctx'=4] {'ctx'}, dimensions={2}, use_global_device_ids=true | all-gather | bytes 655360 | tf_op jit(solution)/shard_map/all_gather | solution.py:135
  70.0 1.3 fusion.34
  71.5 2.8 %fusion.4 = (f32[8,512]{1,0:T(8,128)S(1)}, f32[512,512,8]{1,0,2:T(8,128)S(1)}) fusion(pred[512,512]{0,1:T(8,128)(4,1)S(1)} %fusion.27, bf16[512,8,128]{0,2,1:T(8,128)(2,1)} %bitcast.156, bf16[1,1,512,512]{3,2,1,0:T(8,128)(2,1)} %all-gather, s32[]{:T(128)S(6)} %select_n.16), kind=kOutput, calls=%fused_computation.7 | convolution fusion | flops 543158272 | bytes 9846788 | tf_op jit(solution)/shard_map/qkgd,lkd->kgql/dot_general | solution.py:76
  74.4 3.3 %copy-done.1 = f32[512,512,8]{1,0,2:T(8,128)} copy-done((f32[512,512,8]{1,0,2:T(8,128)}, f32[512,512,8]{1,0,2:T(8,128)S(1)}, u32[]{:S(2)}) %copy-start.1) | copy-done | bytes 8388632
  77.6 2.4 fusion.3
  80.3 1.2 broadcast_in_dim.18.clone
  81.6 5.6 %fusion.22 = f32[512,512]{0,1:T(8,128)} fusion(f32[512,512]{0,1:T(8,128)} %broadcast_in_dim.18.clone, s32[]{:T(128)S(6)} %select_n.16, bf16[512,8,128]{2,1,0:T(8,128)(2,1)S(1)} %bitcast.163, f32[8,512]{1,0:T(8,128)} %fusion.3, f32[8,512]{1,0:T(8,128)S(1)} %get-tuple-element.69, f32[512,512,8]{1,0,2:T(8,128)} %copy-done.1, pred[512,512]{0,1:T(8,128)(4,1)S(1)} %fusion.27), kind=kOutput, calls=%fused_computation.26 | convolution fusion | flops 547356672 | bytes 9994244 | tf_op jit(solution)/shard_map/kgql,qkgd->lkd/dot_general | solution.py:107
  87.8 1.8 copy.111
  89.5 3.0 %copy.104 = f32[512,1,8,128]{0,3,2,1:T(8,128)} copy(f32[512,1,8,128]{3,2,0,1:T(8,128)} %bitcast.159) | data formatting | bytes 4194304 | tf_op jit(solution)/shard_map/convert_element_type | solution.py:93
  92.5 6.9 %fusion.11 = f32[512,8]{0,1:T(8,128)S(1)} fusion(f32[512,1,8,128]{0,3,2,1:T(8,128)} %copy.104, bf16[1,1,512,512]{3,2,1,0:T(8,128)(2,1)S(1)} %copy-done.7, s32[]{:T(128)S(6)} %select_n.16, f32[8,512]{1,0:T(8,128)S(1)} %copy-done.12, f32[8,512]{1,0:T(8,128)S(1)} %get-tuple-element.69, f32[512,512,8]{1,0,2:T(8,128)} %copy-done.1, pred[512,512]{0,1:T(8,128)(4,1)S(1)} %fusion.27), kind=kOutput, calls=%fused_computation.17 | convolution fusion | flops 548401152 | bytes 10928132 | tf_op jit(solution)/shard_map/kgql,lkd->qkgd/dot_general | solution.py:90
  99.4 5.5 %fusion.5 = bf16[8,512,512]{1,2,0:T(8,128)(2,1)S(1)} fusion(f32[8,512]{1,0:T(8,128)S(1)} %bitcast.168, f32[8,512]{1,0:T(8,128)S(1)} %copy-done.12, f32[8,512]{1,0:T(8,128)S(1)} %get-tuple-element.69, f32[512,512,8]{1,0,2:T(8,128)} %copy-done.1, pred[512,512]{0,1:T(8,128)(4,1)S(1)} %fusion.27, bf16[512,8,128]{2,1,0:T(8,128)(2,1)S(1)} %bitcast.164, ...), kind=kOutput, calls=%fused_computation.8 | convolution fusion | flops 551550976 | bytes 14073860 | tf_op jit(solution)/shard_map/qkgd,lkd->kgql/dot_general | solution.py:96
  104.9 1.5 fusion.26
  106.9 1.0 copy-done.4
  107.9 2.3 copy.94
  110.2 3.8 %all-to-all-start.3 = ((bf16[128,4,1024]{0,2,1:T(8,128)(2,1)}), bf16[128,4,1024]{0,2,1:T(8,128)(2,1)S(1)}, u32[]{:S(2)}, u32[]{:S(2)}) async-start(bf16[128,4,1024]{0,2,1:T(8,128)(2,1)} %bitcast.161), calls=%async_computation.5 | async-start | bytes 2097152 | tf_op jit(solution)/shard_map/all_to_all | solution.py:161
  115.0 1.6 convert.8
  116.6 34.8 %reduce-scatter.4.cloned.1.call-done = f32[128,512]{0,1:T(8,128)} async-done(((f32[512,512]{0,1:T(8,128)}), f32[128,512]{0,1:T(8,128)}) %reduce-scatter.4.cloned.1.call-update) | async-done | bytes 262160 | tf_op jit(solution)/shard_map/reduce_scatter | solution.py:157
  151.4 1.0 convert.7
  152.3 1.6 pad_maximum_fusion.1
  154.1 1.3 copy.95
  155.4 29.2 %all-gather.4.cloned.1.call-done = bf16[512,1024]{0,1:T(8,128)(2,1)} async-done(((bf16[128,1024]{0,1:T(8,128)(2,1)}), bf16[512,1024]{0,1:T(8,128)(2,1)}) %all-gather.4.cloned.1.call-update) | async-done | bytes 1048592 | tf_op jit(solution)/shard_map/all_gather | solution.py:162
  184.5 4.7 %convolution_bitcast_fusion = f32[1024,1024]{0,1:T(8,128)} fusion(bf16[512,1024]{0,1:T(8,128)(2,1)} %all-gather.4.cloned.1.call-done, bf16[512,1024]{1,0:T(8,128)(2,1)} %bitcast.165), kind=kOutput, calls=%fused_computation.14 | convolution fusion | flops 1073741824 | bytes 6291456 | tf_op jit(solution)/shard_map/td,tc->dc/dot_general | solution.py:163
  189.3 1.2 copy-done.16
  190.5 2.3 fusion.16
  192.8 4.5 %all-to-all-start.1 = ((bf16[4,128,1024]{2,1,0:T(8,128)(2,1)}), bf16[4,128,1024]{2,1,0:T(8,128)(2,1)}, u32[]{:S(2)}, u32[]{:S(2)}) async-start(bf16[4,128,1024]{2,1,0:T(8,128)(2,1)} %bitcast.30), calls=%async_computation.3 | async-start | bytes 2097152 | tf_op jit(solution)/shard_map/all_to_all | solution.py:169
  197.3 4.4 %multiply_bitcast_fusion.2 = (f32[512,1,8,128]{0,3,2,1:T(8,128)}, f32[512,8,128]{0,2,1:T(8,128)S(1)}) fusion(bf16[8,512,512]{1,2,0:T(8,128)(2,1)} %copy-done.2, bf16[1,1,512,512]{3,2,1,0:T(8,128)(2,1)} %all-gather, s32[]{:T(128)S(6)} %select_n.16), kind=kOutput, calls=%fused_computation.23 | convolution fusion | flops 537395200 | bytes 8519684 | tf_op jit(solution)/shard_map/kgql,lkd->qkgd/dot_general | solution.py:99
  201.9 1.6 maximum_multiply_fusion
  203.5 3.0 %mul.183 = f32[4,128,1024]{1,0,2:T(4,128)} reshape(f32[512,8,128]{0,2,1:T(8,128)} %maximum_multiply_fusion) | data formatting | bytes 4194304 | tf_op jit(solution)/shard_map/mul | solution.py:51
  206.5 2.9 %copy.92 = f32[4,128,1024]{2,1,0:T(8,128)} copy(f32[4,128,1024]{1,0,2:T(4,128)} %mul.183) | data formatting | bytes 4194304 | tf_op jit(solution)/shard_map/mul | solution.py:51
  209.5 3.0 %reshape.284 = f32[4,128,1024]{1,0,2:T(4,128)} reshape(f32[512,1,8,128]{0,3,2,1:T(8,128)} %get-tuple-element.58) | data formatting | bytes 4194304 | tf_op jit(solution)/shard_map/reshape | solution.py:109
  212.5 2.9 %copy.91 = f32[4,128,1024]{2,1,0:T(8,128)} copy(f32[4,128,1024]{1,0,2:T(4,128)} %reshape.284) | data formatting | bytes 4194304 | tf_op jit(solution)/shard_map/reshape | solution.py:109
  215.5 1.5 mul.177
  217.0 2.8 %mul.178 = f32[4,128,1024]{2,1,0:T(8,128)} reshape(f32[512,8,128]{2,1,0:T(8,128)} %mul.177) | data formatting | bytes 4194304 | tf_op jit(solution)/shard_map/mul | solution.py:51
  219.8 3.5 %add_convert_fusion = bf16[4,128,1024]{2,1,0:T(8,128)(2,1)S(1)} fusion(f32[4,128,1024]{2,1,0:T(8,128)} %copy.92, f32[4,128,1024]{2,1,0:T(8,128)} %copy.91, f32[4,128,1024]{2,1,0:T(8,128)} %mul.178), kind=kLoop, calls=%fused_computation.21 | loop fusion | flops 1572864 | bytes 7340032 | tf_op jit(solution)/shard_map/convert_element_type | solution.py:145
  223.2 1.3 copy.93
  224.5 4.8 %all-to-all-start.2 = ((bf16[4,128,1024]{1,2,0:T(8,128)(2,1)}), bf16[4,128,1024]{1,2,0:T(8,128)(2,1)S(1)}, u32[]{:S(2)}, u32[]{:S(2)}) async-start(bf16[4,128,1024]{1,2,0:T(8,128)(2,1)} %copy.93), calls=%async_computation.4 | async-start | bytes 2097152 | tf_op jit(solution)/shard_map/all_to_all | solution.py:148
  229.3 2.3 copy.109
  231.6 1.3 collective-permute-start
  232.9 21.0 %all-to-all-done.2 = bf16[4,128,1024]{1,2,0:T(8,128)(2,1)S(1)} async-done(((bf16[4,128,1024]{1,2,0:T(8,128)(2,1)}), bf16[4,128,1024]{1,2,0:T(8,128)(2,1)S(1)}, u32[]{:S(2)}, u32[]{:S(2)}) %all-to-all-start.2) | async-done | bytes 1048608 | tf_op jit(solution)/shard_map/all_to_all | solution.py:148
  253.9 1.3 copy.96
  255.2 3.2 %multiply_bitcast_fusion = f32[1,1024,512]{1,2,0:T(8,128)} fusion(f32[1024,512]{0,1:T(8,128)} %reduce-scatter.8.cloned.1.call-done), kind=kLoop, calls=%fused_computation.20 | loop fusion | flops 524288 | bytes 4194304 | tf_op jit(solution)/shard_map/broadcast_in_dim | solution.py:172
  258.4 2.9 %copy.97 = f32[1,1024,512]{2,1,0:T(8,128)} copy(f32[1,1024,512]{1,2,0:T(8,128)} %multiply_bitcast_fusion) | data formatting | bytes 4194304
  261.3 2.3 copy.119
  (55 shorter events, 3.1 us)
Async XLA Ops:
  7.2 182.1 %copy-start = (bf16[1,1024,1024]{2,1,0:T(8,128)(2,1)S(1)}, bf16[1,1024,1024]{2,1,0:T(8,128)(2,1)}, u32[]{:S(2)}) copy-start(bf16[1,1024,1024]{2,1,0:T(8,128)(2,1)} %param.23) | copy-start | bytes 6291460
  7.2 11.9 %copy-start.10 = (bf16[1,1,128,512]{3,2,1,0:T(8,128)(2,1)S(1)}, bf16[1,1,128,512]{3,2,1,0:T(8,128)(2,1)}, u32[]{:S(2)}) copy-start(bf16[1,1,128,512]{3,2,1,0:T(8,128)(2,1)} %param.21) | copy-start | bytes 393220
  7.2 46.2 %copy-start.14 = (s32[1,512]{1,0:T(1,128)S(1)}, s32[1,512]{1,0:T(1,128)}, u32[]{:S(2)}) copy-start(s32[1,512]{1,0:T(1,128)} %param.25) | copy-start | bytes 6148
  7.2 46.2 %copy-start.11 = (bf16[1,1,128,512]{3,2,1,0:T(8,128)(2,1)S(1)}, bf16[1,1,128,512]{3,2,1,0:T(8,128)(2,1)}, u32[]{:S(2)}) copy-start(bf16[1,1,128,512]{3,2,1,0:T(8,128)(2,1)} %param.22) | copy-start | bytes 393220
  9.2 60.8 %copy-start.15 = (f32[64]{0:T(128)S(1)}, f32[64]{0:T(128)}, u32[]{:S(2)}) copy-start(f32[64]{0:T(128)} %constant.120) | copy-start | bytes 772
  9.2 62.1 %copy-start.13 = (s32[1,512]{1,0:T(1,128)S(1)}, s32[1,512]{1,0:T(1,128)}, u32[]{:S(2)}) copy-start(s32[1,512]{1,0:T(1,128)} %param.24) | copy-start | bytes 6148
  10.5 69.5 %all-to-all-start = ((bf16[128,4,1024]{2,0,1:T(8,128)(2,1)}), bf16[128,4,1024]{2,0,1:T(8,128)(2,1)S(1)}, u32[]{:S(2)}, u32[]{:S(2)}) async-start(bf16[128,4,1024]{2,0,1:T(8,128)(2,1)} %copy.78), calls=%async_computation | async-start | bytes 2097152 | tf_op jit(solution)/shard_map/all_to_all | solution.py:132
  16.8 98.1 %reduce-scatter.6.cloned.1.call-start = ((), (), s32[]{:S(2)}) async-start(), calls=%async_computation.8 | async-start | bytes 1310720 | tf_op jit(solution)/shard_map/reduce_scatter | solution.py:158
  74.4 3.3 %copy-start.1 = (f32[512,512,8]{1,0,2:T(8,128)}, f32[512,512,8]{1,0,2:T(8,128)S(1)}, u32[]{:S(2)}) copy-start(f32[512,512,8]{1,0,2:T(8,128)S(1)} %get-tuple-element.70) | copy-start | bytes 25165828
  80.3 1.3 copy-start.5
  87.3 64.1 %reduce-scatter.4.cloned.1.call-start = ((), (), s32[]{:S(2)}) async-start(), calls=%async_computation.7 | async-start | bytes 1310720 | tf_op jit(solution)/shard_map/reduce_scatter | solution.py:157
  87.7 4.8 %copy-start.7 = (bf16[1,1,512,512]{3,2,1,0:T(8,128)(2,1)S(1)}, bf16[1,1,512,512]{3,2,1,0:T(8,128)(2,1)}, u32[]{:S(2)}) copy-start(bf16[1,1,512,512]{3,2,1,0:T(8,128)(2,1)} %all-gather.1) | copy-start | bytes 1572868
  87.7 4.8 %copy-start.12 = (f32[8,512]{1,0:T(8,128)S(1)}, f32[8,512]{1,0:T(8,128)}, u32[]{:S(2)}) copy-start(f32[8,512]{1,0:T(8,128)} %fusion.3) | copy-start | bytes 49156
  92.5 6.9 %copy-start.6 = (bf16[64,8,8,128]{3,2,1,0:T(8,128)(2,1)S(1)}, bf16[64,8,8,128]{3,2,1,0:T(8,128)(2,1)}, u32[]{:S(2)}) copy-start(bf16[64,8,8,128]{3,2,1,0:T(8,128)(2,1)} %copy-done.5) | copy-start | bytes 3145732
  99.4 5.5 %copy-start.3 = (bf16[1,1,512,1024]{2,3,1,0:T(8,128)(2,1)S(1)}, bf16[1,1,512,1024]{2,3,1,0:T(8,128)(2,1)}, u32[]{:S(2)}) copy-start(bf16[1,1,512,1024]{2,3,1,0:T(8,128)(2,1)} %copy.108) | copy-start | bytes 3145732
  104.9 2.0 copy-start.2
  104.9 1.6 copy-start.8
  104.9 1.6 copy-start.9
  106.9 1.0 copy-start.4
  110.2 43.9 %all-to-all-start.3 = ((bf16[128,4,1024]{0,2,1:T(8,128)(2,1)}), bf16[128,4,1024]{0,2,1:T(8,128)(2,1)S(1)}, u32[]{:S(2)}, u32[]{:S(2)}) async-start(bf16[128,4,1024]{0,2,1:T(8,128)(2,1)} %bitcast.161), calls=%async_computation.5 | async-start | bytes 2097152 | tf_op jit(solution)/shard_map/all_to_all | solution.py:161
  114.0 70.5 %all-gather.4.cloned.1.call-start = ((), (), s32[]{:S(2)}) async-start(), calls=%async_computation.9 | async-start | bytes 1310720 | tf_op jit(solution)/shard_map/all_gather | solution.py:162
  154.0 101.2 %reduce-scatter.8.cloned.1.call-start = ((), (), s32[]{:S(2)}) async-start(), calls=%async_computation.10 | async-start | bytes 6291456 | tf_op jit(solution)/shard_map/reduce_scatter | solution.py:170
  189.3 1.2 copy-start.16
  192.8 31.8 %all-to-all-start.1 = ((bf16[4,128,1024]{2,1,0:T(8,128)(2,1)}), bf16[4,128,1024]{2,1,0:T(8,128)(2,1)}, u32[]{:S(2)}, u32[]{:S(2)}) async-start(bf16[4,128,1024]{2,1,0:T(8,128)(2,1)} %bitcast.30), calls=%async_computation.3 | async-start | bytes 2097152 | tf_op jit(solution)/shard_map/all_to_all | solution.py:169
  224.5 29.3 %all-to-all-start.2 = ((bf16[4,128,1024]{1,2,0:T(8,128)(2,1)}), bf16[4,128,1024]{1,2,0:T(8,128)(2,1)S(1)}, u32[]{:S(2)}, u32[]{:S(2)}) async-start(bf16[4,128,1024]{1,2,0:T(8,128)(2,1)} %copy.93), calls=%async_computation.4 | async-start | bytes 2097152 | tf_op jit(solution)/shard_map/all_to_all | solution.py:148
  231.6 23.6 %collective-permute-start = (bf16[128,4096]{1,0:T(8,128)(2,1)}, bf16[128,4096]{1,0:T(8,128)(2,1)}, u32[]{:S(2)}, u32[]{:S(2)}) collective-permute-start(bf16[128,4096]{1,0:T(8,128)(2,1)} %bitcast.56), channel_id=1, source_target_pairs={{8,0},{16,8},{24,16},{9,1},{17,9},{25,17},{10,2},{18,10},{26,18},{... | collective-permute-start | bytes 3145736 | tf_op jit(solution)/shard_map/ppermute | solution.py:16
Sparse Core Ops, SparseCore 0:
  87.4 27.5 reduce-scatter.5
  117.9 33.3 reduce-scatter.3
  154.1 30.3 all-gather.3
  189.4 52.6 reduce-scatter.7
where the time goes:
time: 271 us; the launch traced here: 270 us
  waiting for transfers between devices  85.9 us (32%)
  blocking collectives  50.9 us (19%)
  local copies, waits for them, and re-layouts  47.6 us (18%)
  matrix products  33.6 us (12%)
  starting transfers between devices  20.9 us (8%)
  other arithmetic  17 us (6%)
  between operations  14.1 us (5%)
    reduce_scatter x1, waiting for transfers between devices, on_device(): lax.psum_scatter(key_full, 'ctx', scatter_dimension=0, tiled=True)  34.8 us
    all_gather x1, blocking collectives, on_device(): lax.all_gather(key_row_block, 'ctx', axis=0, tiled=True)  34.3 us
    all_gather x1, waiting for transfers between devices, on_device(): gradient_total = lax.all_gather(kv_grad, 'ctx', axis=0, tiled=True)  29.2 us
    all_to_all x1, waiting for transfers between devices, on_device(): lax.all_to_all(query_back, 'ctx', split_axis=0, concat_axis=1, tiled=True)  21 us
    unnamed x40, local copies, waits for them, and re-layouts  16.7 us
    all_gather x1, blocking collectives, on_device(): lax.all_gather(value_row_block, 'ctx', axis=0, tiled=True)  16.6 us
    mul x4, local copies, waits for them, and re-layouts, rotate_back(): return gradient * cosine + turned * sine_term  10.2 us
    dot_general x1, matrix products, attend_local(): jnp.einsum('kgql,lkd->qkgd', probs_half, v_blk, preferred_element_type=jn...  6.9 us
  transfers between devices with their start and end apart: 9, of which 4 were waited for; matrix products, arithmetic and copies ran while one was open for 25% of the time, Pallas kernels for 0%

commit v1 on v0

--- a/solution.py
+++ b/solution.py
@@ -8,6 +8,12 @@
 QUERY_HEADS = 32
 KEY_VALUE_HEADS = 4
 HEAD_WIDTH = 128
+
+
+def in_order(blocks, dim):
+    dims = list(blocks.shape[1:])
+    dims[dim] *= blocks.shape[0]
+    return jnp.moveaxis(blocks, 0, dim).reshape(dims)
 
 
 def passed_along(value, axis, by):
@@ -159,7 +165,19 @@
     )
     kv_grad = jnp.concatenate([key_sum, value_sum], 1).astype(jnp.bfloat16)
     input_cols = lax.all_to_all(inputs, "ctx", split_axis=1, concat_axis=0, tiled=True)
-    gradient_total = lax.all_gather(kv_grad, "ctx", axis=0, tiled=True)
+    devices = lax.axis_size("ctx")
+    pairs_2 = [(i_2, (i_2 + 1) % devices) for i_2 in range(devices)]
+    back = [(b, a) for a, b in pairs_2]
+    lower, upper = ([], [])
+    for step in range(devices - 1):
+        if step % 2 == 0:
+            lower.append(lax.ppermute(lower[-1] if lower else kv_grad, "ctx", pairs_2))
+        else:
+            upper.append(lax.ppermute(upper[-1] if upper else kv_grad, "ctx", back))
+    blocks = jnp.stack([*lower[::-1], kv_grad, *upper])
+    shift = lax.axis_index("ctx") - len(lower)
+    blocks = blocks[(jnp.arange(devices) - shift) % devices]
+    gradient_total = in_order(blocks, 0)
     rows_part = jnp.einsum(
         "td,tc->dc", input_cols, gradient_total, preferred_element_type=jnp.float32
     )

time: 271 us -> 261 us (0.963)
  waiting for transfers between devices: 85.9 us -> 65.3 us
  starting transfers between devices: 20.9 us -> 29.3 us
    all_gather x1 -> x0, waiting for transfers between devices: 29.2 us -> none  [on_device(): gradient_total = lax.all_gather(kv_grad, 'ctx', axis=0, tiled=True)]
    ppermute x0 -> x3, waiting for transfers between devices: none -> 11.3 us  [the longest x2 11.3 us: on_device(): lower.append(lax.ppermute(lower[-1] if lower else kv_grad, 'ctx', pairs_2))]
    ppermute x0 -> x3, starting transfers between devices: none -> 7.59 us  [the longest x2 6.55 us: on_device(): lower.append(lax.ppermute(lower[-1] if lower else kv_grad, 'ctx', pairs_2))]
    unnamed x40 -> x42, local copies, waits for them, and re-layouts: 16.7 us -> 16.6 us
  transfers between devices with their start and end apart: 9 -> 11, of which waited for: 4 -> 4; matrix products, arithmetic and copies ran while one was open for 25% -> 27% of each run, Pallas kernels for 0% -> 0%
where the time goes in v1:
time: 261 us; the launch traced here: 260 us
  waiting for transfers between devices  65.3 us (25%)
  blocking collectives  50.9 us (20%)
  local copies, waits for them, and re-layouts  49.3 us (19%)
  matrix products  33.6 us (13%)
  starting transfers between devices  29.3 us (11%)
  other arithmetic  17.7 us (7%)
  between operations  14.1 us (5%)
    all_gather x1, blocking collectives, on_device(): lax.all_gather(key_row_block, 'ctx', axis=0, tiled=True)  34.3 us
    reduce_scatter x1, waiting for transfers between devices, on_device(): lax.psum_scatter(key_full, 'ctx', scatter_dimension=0, tiled=True)  33.3 us
    all_to_all x1, waiting for transfers between devices, on_device(): lax.all_to_all(query_back, 'ctx', split_axis=0, concat_axis=1, tiled=True)  20.6 us
    all_gather x1, blocking collectives, on_device(): lax.all_gather(value_row_block, 'ctx', axis=0, tiled=True)  16.6 us
    unnamed x42, local copies, waits for them, and re-layouts  16.6 us
    ppermute x2, waiting for transfers between devices, on_device(): lower.append(lax.ppermute(lower[-1] if lower else kv_grad, 'ctx', pairs_2))  11.3 us
    mul x4, local copies, waits for them, and re-layouts, rotate_back(): return gradient * cosine + turned * sine_term  10.1 us
    dot_general x1, matrix products, attend_local(): jnp.einsum('kgql,lkd->qkgd', probs_half, v_blk, preferred_element_type=jn...  6.89 us
  transfers between devices with their start and end apart: 11, of which 4 were waited for; matrix products, arithmetic and copies ran while one was open for 27% of the time, Pallas kernels for 0%

profile of v1, /device:TPU:0, one launch (start us, length us, event | category | flops | bytes accessed | tf_op | source)
XLA Modules:
  0.0 260.2 jit_solution(17814629390102036821)
XLA Ops:
  7.2 2.0 all_to_all.48
  9.2 1.3 copy.83
  10.5 6.3 %all-to-all-start = ((bf16[128,4,1024]{2,0,1:T(8,128)(2,1)}), bf16[128,4,1024]{2,0,1:T(8,128)(2,1)S(1)}, u32[]{:S(2)}, u32[]{:S(2)}) async-start(bf16[128,4,1024]{2,0,1:T(8,128)(2,1)} %copy.83), calls=%async_computation | async-start | bytes 2097152 | tf_op jit(solution)/shard_map/all_to_all | solution.py:138
  16.8 2.3 copy.113
  19.1 34.3 %all-gather = bf16[1,1,512,512]{3,2,1,0:T(8,128)(2,1)} all-gather(bf16[1,1,128,512]{3,2,1,0:T(8,128)(2,1)S(1)} %copy-done.12), channel_id=2, replica_groups=mesh['section'=4,'dp'=2,'ctx'=4] {'ctx'}, dimensions={2}, use_global_device_ids=true | all-gather | bytes 655360 | tf_op jit(solution)/shard_map/all_gather | solution.py:140
  53.4 16.6 %all-gather.1 = bf16[1,1,512,512]{3,2,1,0:T(8,128)(2,1)} all-gather(bf16[1,1,128,512]{3,2,1,0:T(8,128)(2,1)S(1)} %copy-done.13), channel_id=3, replica_groups=mesh['section'=4,'dp'=2,'ctx'=4] {'ctx'}, dimensions={2}, use_global_device_ids=true | all-gather | bytes 655360 | tf_op jit(solution)/shard_map/all_gather | solution.py:141
  70.1 1.3 fusion.34
  71.5 2.8 %fusion.4 = (f32[8,512]{1,0:T(8,128)S(1)}, f32[512,512,8]{1,0,2:T(8,128)S(1)}) fusion(pred[512,512]{0,1:T(8,128)(4,1)S(1)} %fusion.28, bf16[512,8,128]{0,2,1:T(8,128)(2,1)} %bitcast.166, bf16[1,1,512,512]{3,2,1,0:T(8,128)(2,1)} %all-gather, s32[]{:T(128)S(6)} %select_n.39), kind=kOutput, calls=%fused_computation.8 | convolution fusion | flops 543158272 | bytes 9846788 | tf_op jit(solution)/shard_map/qkgd,lkd->kgql/dot_general | solution.py:82
  74.4 3.3 %copy-done.1 = f32[512,512,8]{1,0,2:T(8,128)} copy-done((f32[512,512,8]{1,0,2:T(8,128)}, f32[512,512,8]{1,0,2:T(8,128)S(1)}, u32[]{:S(2)}) %copy-start.1) | copy-done | bytes 8388632
  77.6 2.4 fusion.3
  80.3 1.2 broadcast_in_dim.18.clone
  81.6 5.4 %fusion.22 = f32[512,512]{1,0:T(8,128)} fusion(f32[512,512]{1,0:T(8,128)} %broadcast_in_dim.18.clone, s32[]{:T(128)S(6)} %select_n.39, bf16[512,8,128]{2,1,0:T(8,128)(2,1)S(1)} %bitcast.174, f32[8,512]{1,0:T(8,128)} %fusion.3, f32[8,512]{1,0:T(8,128)S(1)} %get-tuple-element.67, f32[512,512,8]{1,0,2:T(8,128)} %copy-done.1, pred[512,512]{0,1:T(8,128)(4,1)S(1)} %fusion.28), kind=kOutput, calls=%fused_computation.27 | convolution fusion | flops 547356672 | bytes 9994244 | tf_op jit(solution)/shard_map/kgql,qkgd->lkd/dot_general | solution.py:113
  87.6 1.8 copy.116
  89.4 3.0 %copy.110 = f32[512,1,8,128]{0,3,2,1:T(8,128)} copy(f32[512,1,8,128]{3,2,0,1:T(8,128)} %bitcast.169) | data formatting | bytes 4194304 | tf_op jit(solution)/shard_map/convert_element_type | solution.py:99
  92.4 6.9 %fusion.11 = f32[512,8]{0,1:T(8,128)S(1)} fusion(f32[512,1,8,128]{0,3,2,1:T(8,128)} %copy.110, bf16[1,1,512,512]{3,2,1,0:T(8,128)(2,1)S(1)} %copy-done.8, s32[]{:T(128)S(6)} %select_n.39, f32[8,512]{1,0:T(8,128)S(1)} %copy-done.14, f32[8,512]{1,0:T(8,128)S(1)} %get-tuple-element.67, f32[512,512,8]{1,0,2:T(8,128)} %copy-done.1, pred[512,512]{0,1:T(8,128)(4,1)S(1)} %fusion.28), kind=kOutput, calls=%fused_computation.18 | convolution fusion | flops 548401152 | bytes 10928132 | tf_op jit(solution)/shard_map/kgql,lkd->qkgd/dot_general | solution.py:96
  99.3 5.5 %fusion.5 = bf16[8,512,512]{1,2,0:T(8,128)(2,1)S(1)} fusion(f32[8,512]{1,0:T(8,128)S(1)} %bitcast.181, f32[8,512]{1,0:T(8,128)S(1)} %copy-done.14, f32[8,512]{1,0:T(8,128)S(1)} %get-tuple-element.67, f32[512,512,8]{1,0,2:T(8,128)} %copy-done.1, pred[512,512]{0,1:T(8,128)(4,1)S(1)} %fusion.28, bf16[512,8,128]{2,1,0:T(8,128)(2,1)S(1)} %bitcast.175, ...), kind=kOutput, calls=%fused_computation.9 | convolution fusion | flops 551550976 | bytes 14073860 | tf_op jit(solution)/shard_map/qkgd,lkd->kgql/dot_general | solution.py:102
  104.8 2.0 copy-done.2
  106.8 1.4 fusion.26
  109.6 1.6 copy.99
  111.3 1.3 copy.100
  112.6 4.3 %all-to-all-start.3 = ((bf16[128,4,1024]{2,0,1:T(8,128)(2,1)}), bf16[128,4,1024]{2,0,1:T(8,128)(2,1)}, u32[]{:S(2)}, u32[]{:S(2)}) async-start(bf16[128,4,1024]{2,0,1:T(8,128)(2,1)} %copy.100), calls=%async_computation.5 | async-start | bytes 2097152 | tf_op jit(solution)/shard_map/all_to_all | solution.py:167
  117.9 33.3 %reduce-scatter.4.cloned.1.call-done = f32[128,512]{1,0:T(8,128)} async-done(((f32[512,512]{1,0:T(8,128)}), f32[128,512]{1,0:T(8,128)}) %reduce-scatter.4.cloned.1.call-update) | async-done | bytes 262160 | tf_op jit(solution)/shard_map/reduce_scatter | solution.py:163
  152.2 2.9 %collective-permute-start = (bf16[128,1024]{1,0:T(8,128)(2,1)S(1)}, bf16[128,1024]{1,0:T(8,128)(2,1)S(1)}, u32[]{:S(2)}, u32[]{:S(2)}) collective-permute-start(bf16[128,1024]{1,0:T(8,128)(2,1)S(1)} %pad_maximum_fusion.2), channel_id=1, source_target_pairs={{0,1},{1,2},{2,3},{3,0},{4,5},{5,6},{6,7},{7,4},{8,9},{9,10},{10,1... | collective-permute-start | bytes 786440 | tf_op jit(solution)/shard_map/ppermute | solution.py:174
  156.2 7.2 %collective-permute-done = bf16[128,1024]{1,0:T(8,128)(2,1)S(1)} collective-permute-done((bf16[128,1024]{1,0:T(8,128)(2,1)S(1)}, bf16[128,1024]{1,0:T(8,128)(2,1)S(1)}, u32[]{:S(2)}, u32[]{:S(2)}) %collective-permute-start) | collective-permute-done | bytes 262176 | tf_op jit(solution)/shard_map/ppermute | solution.py:174
  163.3 3.7 %collective-permute-start.1 = (bf16[128,1024]{1,0:T(8,128)(2,1)S(1)}, bf16[128,1024]{1,0:T(8,128)(2,1)S(1)}, u32[]{:S(2)}, u32[]{:S(2)}) collective-permute-start(bf16[128,1024]{1,0:T(8,128)(2,1)S(1)} %collective-permute-done), channel_id=1, source_target_pairs={{0,1},{1,2},{2,3},{3,0},{4,5},{5,6},{6,7},{7,4},{8,9},{9,10},{10,1... | collective-permute-start | bytes 786440 | tf_op jit(solution)/shard_map/ppermute | solution.py:174
  168.9 4.1 %collective-permute-done.1 = bf16[128,1024]{1,0:T(8,128)(2,1)S(1)} collective-permute-done((bf16[128,1024]{1,0:T(8,128)(2,1)S(1)}, bf16[128,1024]{1,0:T(8,128)(2,1)S(1)}, u32[]{:S(2)}, u32[]{:S(2)}) %collective-permute-start.1) | collective-permute-done | bytes 262176 | tf_op jit(solution)/shard_map/ppermute | solution.py:174
  174.1 1.6 gather_fusion
  175.7 4.9 %convolution_bitcast_fusion = f32[1024,1024]{0,1:T(8,128)} fusion(bf16[4,128,1024]{2,1,0:T(8,128)(2,1)} %gather_fusion, bf16[128,4,1024]{2,0,1:T(8,128)(2,1)} %all-to-all-done.3), kind=kOutput, calls=%fused_computation.15 | convolution fusion | flops 1073741824 | bytes 6291456 | tf_op jit(solution)/shard_map/td,tc->dc/dot_general | solution.py:181
  180.6 2.3 fusion.16
  182.9 4.5 %all-to-all-start.1 = ((bf16[4,128,1024]{2,1,0:T(8,128)(2,1)}), bf16[4,128,1024]{2,1,0:T(8,128)(2,1)}, u32[]{:S(2)}, u32[]{:S(2)}) async-start(bf16[4,128,1024]{2,1,0:T(8,128)(2,1)} %bitcast.173), calls=%async_computation.3 | async-start | bytes 2097152 | tf_op jit(solution)/shard_map/all_to_all | solution.py:187
  187.6 1.5 mul.177
  189.1 2.7 %mul.178 = f32[4,128,1024]{2,1,0:T(8,128)} reshape(f32[512,8,128]{2,1,0:T(8,128)} %mul.177) | data formatting | bytes 4194304 | tf_op jit(solution)/shard_map/mul | solution.py:57
  191.8 4.4 %multiply_bitcast_fusion.2 = (f32[512,1,8,128]{0,3,2,1:T(8,128)}, f32[512,8,128]{0,2,1:T(8,128)S(1)}) fusion(bf16[8,512,512]{1,2,0:T(8,128)(2,1)} %copy-done.2, bf16[1,1,512,512]{3,2,1,0:T(8,128)(2,1)} %all-gather, s32[]{:T(128)S(6)} %select_n.39), kind=kOutput, calls=%fused_computation.24 | convolution fusion | flops 537395200 | bytes 8519684 | tf_op jit(solution)/shard_map/kgql,lkd->qkgd/dot_general | solution.py:105
  196.4 1.6 maximum_multiply_fusion
  198.0 3.0 %mul.183 = f32[4,128,1024]{1,0,2:T(4,128)} reshape(f32[512,8,128]{0,2,1:T(8,128)} %maximum_multiply_fusion) | data formatting | bytes 4194304 | tf_op jit(solution)/shard_map/mul | solution.py:57
  201.0 2.9 %copy.97 = f32[4,128,1024]{2,1,0:T(8,128)} copy(f32[4,128,1024]{1,0,2:T(4,128)} %mul.183) | data formatting | bytes 4194304 | tf_op jit(solution)/shard_map/mul | solution.py:57
  203.9 3.0 %reshape.368 = f32[4,128,1024]{1,0,2:T(4,128)} reshape(f32[512,1,8,128]{0,3,2,1:T(8,128)} %get-tuple-element.58) | data formatting | bytes 4194304 | tf_op jit(solution)/shard_map/reshape | solution.py:115
  206.9 3.0 %copy.96 = f32[4,128,1024]{2,1,0:T(8,128)} copy(f32[4,128,1024]{1,0,2:T(4,128)} %reshape.368) | data formatting | bytes 4194304 | tf_op jit(solution)/shard_map/reshape | solution.py:115
  210.0 3.4 %add_convert_fusion = bf16[4,128,1024]{2,1,0:T(8,128)(2,1)S(1)} fusion(f32[4,128,1024]{2,1,0:T(8,128)} %copy.97, f32[4,128,1024]{2,1,0:T(8,128)} %copy.96, f32[4,128,1024]{2,1,0:T(8,128)} %mul.178), kind=kLoop, calls=%fused_computation.22 | loop fusion | flops 1572864 | bytes 7340032 | tf_op jit(solution)/shard_map/convert_element_type | solution.py:151
  213.4 1.3 copy.98
  214.7 5.1 %all-to-all-start.2 = ((bf16[4,128,1024]{1,2,0:T(8,128)(2,1)}), bf16[4,128,1024]{1,2,0:T(8,128)(2,1)S(1)}, u32[]{:S(2)}, u32[]{:S(2)}) async-start(bf16[4,128,1024]{1,2,0:T(8,128)(2,1)} %copy.98), calls=%async_computation.4 | async-start | bytes 2097152 | tf_op jit(solution)/shard_map/all_to_all | solution.py:154
  219.8 2.3 copy.114
  222.1 1.3 collective-permute-start.3
  223.4 20.6 %all-to-all-done.2 = bf16[4,128,1024]{1,2,0:T(8,128)(2,1)S(1)} async-done(((bf16[4,128,1024]{1,2,0:T(8,128)(2,1)}), bf16[4,128,1024]{1,2,0:T(8,128)(2,1)S(1)}, u32[]{:S(2)}, u32[]{:S(2)}) %all-to-all-start.2) | async-done | bytes 1048608 | tf_op jit(solution)/shard_map/all_to_all | solution.py:154
  244.0 1.3 copy.102
  245.3 3.2 %multiply_bitcast_fusion = f32[1,1024,512]{1,2,0:T(8,128)} fusion(f32[1024,512]{0,1:T(8,128)} %reduce-scatter.8.cloned.1.call-done), kind=kLoop, calls=%fused_computation.21 | loop fusion | flops 524288 | bytes 4194304 | tf_op jit(solution)/shard_map/broadcast_in_dim | solution.py:190
  248.5 2.9 %copy.103 = f32[1,1024,512]{2,1,0:T(8,128)} copy(f32[1,1024,512]{1,2,0:T(8,128)} %multiply_bitcast_fusion) | data formatting | bytes 4194304
  251.4 2.3 copy.124
  (68 shorter events, 9.1 us)
Async XLA Ops:
  7.2 173.5 %copy-start = (bf16[1,1024,1024]{2,1,0:T(8,128)(2,1)S(1)}, bf16[1,1024,1024]{2,1,0:T(8,128)(2,1)}, u32[]{:S(2)}) copy-start(bf16[1,1024,1024]{2,1,0:T(8,128)(2,1)} %param.23) | copy-start | bytes 6291460
  7.2 11.9 %copy-start.12 = (bf16[1,1,128,512]{3,2,1,0:T(8,128)(2,1)S(1)}, bf16[1,1,128,512]{3,2,1,0:T(8,128)(2,1)}, u32[]{:S(2)}) copy-start(bf16[1,1,128,512]{3,2,1,0:T(8,128)(2,1)} %param.21) | copy-start | bytes 393220
  7.2 46.2 %copy-start.13 = (bf16[1,1,128,512]{3,2,1,0:T(8,128)(2,1)S(1)}, bf16[1,1,128,512]{3,2,1,0:T(8,128)(2,1)}, u32[]{:S(2)}) copy-start(bf16[1,1,128,512]{3,2,1,0:T(8,128)(2,1)} %param.22) | copy-start | bytes 393220
  9.2 60.8 %copy-start.16 = (s32[1,512]{1,0:T(1,128)S(1)}, s32[1,512]{1,0:T(1,128)}, u32[]{:S(2)}) copy-start(s32[1,512]{1,0:T(1,128)} %param.25) | copy-start | bytes 6148
  9.2 60.8 %copy-start.17 = (f32[64]{0:T(128)S(1)}, f32[64]{0:T(128)}, u32[]{:S(2)}) copy-start(f32[64]{0:T(128)} %constant.138) | copy-start | bytes 772
  9.2 62.1 %copy-start.15 = (s32[1,512]{1,0:T(1,128)S(1)}, s32[1,512]{1,0:T(1,128)}, u32[]{:S(2)}) copy-start(s32[1,512]{1,0:T(1,128)} %param.24) | copy-start | bytes 6148
  10.5 69.5 %all-to-all-start = ((bf16[128,4,1024]{2,0,1:T(8,128)(2,1)}), bf16[128,4,1024]{2,0,1:T(8,128)(2,1)S(1)}, u32[]{:S(2)}, u32[]{:S(2)}) async-start(bf16[128,4,1024]{2,0,1:T(8,128)(2,1)} %copy.83), calls=%async_computation | async-start | bytes 2097152 | tf_op jit(solution)/shard_map/all_to_all | solution.py:138
  16.8 100.1 %reduce-scatter.6.cloned.1.call-start = ((), (), s32[]{:S(2)}) async-start(), calls=%async_computation.8 | async-start | bytes 1310720 | tf_op jit(solution)/shard_map/reduce_scatter | solution.py:164
  74.4 3.3 %copy-start.1 = (f32[512,512,8]{1,0,2:T(8,128)}, f32[512,512,8]{1,0,2:T(8,128)S(1)}, u32[]{:S(2)}) copy-start(f32[512,512,8]{1,0,2:T(8,128)S(1)} %get-tuple-element.68) | copy-start | bytes 25165828
  80.3 1.4 copy-start.6
  87.1 64.1 %reduce-scatter.4.cloned.1.call-start = ((), (), s32[]{:S(2)}) async-start(), calls=%async_computation.7 | async-start | bytes 1310720 | tf_op jit(solution)/shard_map/reduce_scatter | solution.py:163
  87.6 4.8 %copy-start.8 = (bf16[1,1,512,512]{3,2,1,0:T(8,128)(2,1)S(1)}, bf16[1,1,512,512]{3,2,1,0:T(8,128)(2,1)}, u32[]{:S(2)}) copy-start(bf16[1,1,512,512]{3,2,1,0:T(8,128)(2,1)} %all-gather.1) | copy-start | bytes 1572868
  87.6 4.8 %copy-start.14 = (f32[8,512]{1,0:T(8,128)S(1)}, f32[8,512]{1,0:T(8,128)}, u32[]{:S(2)}) copy-start(f32[8,512]{1,0:T(8,128)} %fusion.3) | copy-start | bytes 49156
  92.3 6.9 %copy-start.7 = (bf16[64,8,8,128]{3,2,1,0:T(8,128)(2,1)S(1)}, bf16[64,8,8,128]{3,2,1,0:T(8,128)(2,1)}, u32[]{:S(2)}) copy-start(bf16[64,8,8,128]{3,2,1,0:T(8,128)(2,1)} %copy-done.6) | copy-start | bytes 3145732
  99.3 7.5 %copy-start.3 = (bf16[1,1,512,1024]{2,3,1,0:T(8,128)(2,1)S(1)}, bf16[1,1,512,1024]{2,3,1,0:T(8,128)(2,1)}, u32[]{:S(2)}) copy-start(bf16[1,1,512,1024]{2,3,1,0:T(8,128)(2,1)} %copy.113) | copy-start | bytes 3145732
  104.7 2.0 copy-start.2
  106.8 1.5 copy-start.10
  108.6 1.0 copy-start.4
  112.6 63.1 %all-to-all-start.3 = ((bf16[128,4,1024]{2,0,1:T(8,128)(2,1)}), bf16[128,4,1024]{2,0,1:T(8,128)(2,1)}, u32[]{:S(2)}, u32[]{:S(2)}) async-start(bf16[128,4,1024]{2,0,1:T(8,128)(2,1)} %copy.100), calls=%async_computation.5 | async-start | bytes 2097152 | tf_op jit(solution)/shard_map/all_to_all | solution.py:167
  116.9 128.5 %reduce-scatter.8.cloned.1.call-start = ((), (), s32[]{:S(2)}) async-start(), calls=%async_computation.9 | async-start | bytes 6291456 | tf_op jit(solution)/shard_map/reduce_scatter | solution.py:188
  152.2 11.1 %collective-permute-start = (bf16[128,1024]{1,0:T(8,128)(2,1)S(1)}, bf16[128,1024]{1,0:T(8,128)(2,1)S(1)}, u32[]{:S(2)}, u32[]{:S(2)}) collective-permute-start(bf16[128,1024]{1,0:T(8,128)(2,1)S(1)} %pad_maximum_fusion.2), channel_id=1, source_target_pairs={{0,1},{1,2},{2,3},{3,0},{4,5},{5,6},{6,7},{7,4},{8,9},{9,10},{10,1... | collective-permute-start | bytes 786440 | tf_op jit(solution)/shard_map/ppermute | solution.py:174
  155.1 13.8 %collective-permute-start.2 = (bf16[128,1024]{1,0:T(8,128)(2,1)S(1)}, bf16[128,1024]{1,0:T(8,128)(2,1)S(1)}, u32[]{:S(2)}, u32[]{:S(2)}) collective-permute-start(bf16[128,1024]{1,0:T(8,128)(2,1)S(1)} %pad_maximum_fusion.2), channel_id=1, source_target_pairs={{1,0},{2,1},{3,2},{0,3},{5,4},{6,5},{7,6},{4,7},{9,8},{10,9},{11,1... | collective-permute-start | bytes 786440 | tf_op jit(solution)/shard_map/ppermute | solution.py:176
  163.3 9.8 %copy-start.11 = (bf16[128,1024]{1,0:T(8,128)(2,1)}, bf16[128,1024]{1,0:T(8,128)(2,1)S(1)}, u32[]{:S(2)}) copy-start(bf16[128,1024]{1,0:T(8,128)(2,1)S(1)} %collective-permute-done) | copy-start | bytes 786436
  163.3 9.8 %collective-permute-start.1 = (bf16[128,1024]{1,0:T(8,128)(2,1)S(1)}, bf16[128,1024]{1,0:T(8,128)(2,1)S(1)}, u32[]{:S(2)}, u32[]{:S(2)}) collective-permute-start(bf16[128,1024]{1,0:T(8,128)(2,1)S(1)} %collective-permute-done), channel_id=1, source_target_pairs={{0,1},{1,2},{2,3},{3,0},{4,5},{5,6},{6,7},{7,4},{8,9},{9,10},{10,1... | collective-permute-start | bytes 786440 | tf_op jit(solution)/shard_map/ppermute | solution.py:174
  175.7 4.9 %copy-start.5 = (bf16[4,128,1024]{2,1,0:T(8,128)(2,1)S(1)}, bf16[4,128,1024]{2,1,0:T(8,128)(2,1)}, u32[]{:S(2)}) copy-start(bf16[4,128,1024]{2,1,0:T(8,128)(2,1)} %gather_fusion) | copy-start | bytes 3145732
  180.6 6.8 %copy-start.9 = (f32[512,64]{0,1:T(8,128)S(1)}, f32[512,64]{0,1:T(8,128)}, u32[]{:S(2)}) copy-start(f32[512,64]{0,1:T(8,128)} %get-tuple-element.64) | copy-start | bytes 393220
  182.9 31.8 %all-to-all-start.1 = ((bf16[4,128,1024]{2,1,0:T(8,128)(2,1)}), bf16[4,128,1024]{2,1,0:T(8,128)(2,1)}, u32[]{:S(2)}, u32[]{:S(2)}) async-start(bf16[4,128,1024]{2,1,0:T(8,128)(2,1)} %bitcast.173), calls=%async_computation.3 | async-start | bytes 2097152 | tf_op jit(solution)/shard_map/all_to_all | solution.py:187
  214.7 29.3 %all-to-all-start.2 = ((bf16[4,128,1024]{1,2,0:T(8,128)(2,1)}), bf16[4,128,1024]{1,2,0:T(8,128)(2,1)S(1)}, u32[]{:S(2)}, u32[]{:S(2)}) async-start(bf16[4,128,1024]{1,2,0:T(8,128)(2,1)} %copy.98), calls=%async_computation.4 | async-start | bytes 2097152 | tf_op jit(solution)/shard_map/all_to_all | solution.py:154
  222.1 23.2 %collective-permute-start.3 = (bf16[128,4096]{1,0:T(8,128)(2,1)}, bf16[128,4096]{1,0:T(8,128)(2,1)}, u32[]{:S(2)}, u32[]{:S(2)}) collective-permute-start(bf16[128,4096]{1,0:T(8,128)(2,1)} %bitcast.64), channel_id=1, source_target_pairs={{8,0},{16,8},{24,16},{9,1},{17,9},{25,17},{10,2},{18,10},{26,18},{... | collective-permute-start | bytes 3145736 | tf_op jit(solution)/shard_map/ppermute | solution.py:22
Sparse Core Ops, SparseCore 0:
  87.2 27.2 reduce-scatter.5
  117.4 33.7 reduce-scatter.3
  180.7 55.1 reduce-scatter.7
